TPU v7x, 1024 devices: a whole 4x4x32 slice. The times are simulated.
1024 devices in a mesh: ctx: 256 (over z, y, core), head: 4 (over x).
Axes of the slice: x: 4, y: 4, z: 32, core: 2. Of those that a mesh axis runs over, the one named last changes fastest.
Arguments:
- queries: bfloat16 [65536, 4096], P('ctx', 'head'), parts along dimension 1, may hold values from -4.6 to 4.6
- key_vectors: bfloat16 [65536, 512], P('ctx', 'head'), parts along dimension 1, may hold values from -4.6 to 4.6
- value_vectors: bfloat16 [65536, 512], P('ctx', 'head'), parts along dimension 1, may hold values from -6 to 6
- doc_ids: int32 [65536], replicated, may hold values from 0 to 169, never falling along the last dimension, each value on 1 to 768 neighbouring positions
- grad_out: bfloat16 [65536, 4096], P('ctx', 'head'), parts along dimension 1, may hold values from -6 to 6
Outputs:
- attended: bfloat16 [65536, 4096], P('ctx', 'head'), parts along dimension 1
- grad_query: bfloat16 [65536, 4096], P('ctx', 'head'), parts along dimension 1
- grad_key: bfloat16 [65536, 512], P('ctx', 'head'), parts along dimension 1
- grad_value: bfloat16 [65536, 512], P('ctx', 'head'), parts along dimension 1
There are 4 independent parts, one for each index of `head`. A program takes and returns all parts, laid end to end along the dimension named above; an argument that names none is the same for every part. Nothing has to cross between parts.
Inputs may be any that keep to these rules, and one draw needn't show every extreme that they name: doc_ids never fall along the sequence; each document holds 1 to 768 positions and one holds exactly 768.
All inputs are finite; a program needn't handle non-finite values.
Results may differ from a plain program's by a relative error of at most 0.029.
Values may be sent and summed in bfloat16 or wider, within the bound.
A program may use at most 32 MiB of HBM per device.

v0:
```python
import jax
import jax.numpy as jnp
from jax import lax
from jax.sharding import PartitionSpec as P

REACH = 3


def from_behind(value, axis, by):
    size = lax.axis_size(axis)
    pairs = [(i, i + by) for i in range(size) if 0 <= i + by < size]
    return lax.ppermute(value, axis, pairs)


def block_grads(query_rows, grad_rows, key_value, query_pos, key_pos, query_doc, key_doc):
    row_count = query_rows.shape[0]
    head_dim = key_value.shape[1] // 2
    score_scale = head_dim ** (-0.5)
    query_heads = query_rows.reshape(row_count, -1, head_dim)
    grad_heads = grad_rows.reshape(row_count, -1, head_dim)
    key_part = key_value[:, :head_dim]
    value_part = key_value[:, head_dim:]
    allowed = (
        (query_doc[:, None] == key_doc[None, :])
        & (key_pos[None, :] <= query_pos[:, None])
        & (key_pos[None, :] >= 0)
    )
    scores = (
        jnp.einsum("thd,kd->htk", query_heads, key_part, preferred_element_type=jnp.float32)
        * score_scale
    )
    scores = jnp.where(allowed[None], scores, -1e30)
    row_max = jnp.max(scores, axis=-1, keepdims=True)
    row_sum = jnp.sum(
        jnp.where(allowed[None], jnp.exp(scores - row_max), 0.0), axis=-1, keepdims=True
    )
    log_norm = row_max + jnp.log(row_sum)
    probs = jnp.where(allowed[None], jnp.exp(scores - log_norm), 0.0)
    weights = probs.astype(jnp.bfloat16)
    attended = jnp.einsum(
        "htk,kd->thd", weights, value_part, preferred_element_type=jnp.float32
    ).astype(jnp.bfloat16)
    delta = jnp.sum(grad_heads.astype(jnp.float32) * attended.astype(jnp.float32), axis=-1)
    grad_prob = jnp.einsum(
        "thd,kd->htk", grad_heads, value_part, preferred_element_type=jnp.float32
    )
    dscore = (probs * (grad_prob - jnp.transpose(delta)[:, :, None])).astype(jnp.bfloat16)
    grad_query = (
        jnp.einsum("htk,kd->thd", dscore, key_part, preferred_element_type=jnp.float32)
        * score_scale
    ).astype(jnp.bfloat16)
    grad_key = (
        jnp.einsum("htk,thd->kd", dscore, query_heads, preferred_element_type=jnp.float32)
        * score_scale
    )
    grad_value = jnp.einsum("htk,thd->kd", weights, grad_heads, preferred_element_type=jnp.float32)
    return (
        attended.reshape(row_count, -1),
        grad_query.reshape(row_count, -1),
        jnp.concatenate([grad_key, grad_value], axis=1),
    )


def body(queries, key_vectors, value_vectors, doc_ids, grad_out):
    row_count = queries.shape[0]
    head_dim = key_vectors.shape[1]
    key_span = (REACH + 1) * row_count
    first_row = lax.axis_index("ctx") * row_count
    key_value = jnp.concatenate([key_vectors, value_vectors], axis=1)
    held_blocks = [key_value]
    visiting = key_value
    for repeat in range(REACH):
        visiting = from_behind(visiting, "ctx", 1)
        held_blocks.append(visiting)
    stacked = jnp.stack(held_blocks)
    window = stacked[::-1].reshape(key_span, 2 * head_dim)
    padded_doc = jnp.concatenate([jnp.full((REACH * row_count,), -1, jnp.int32), doc_ids], axis=0)
    key_doc = lax.dynamic_slice_in_dim(padded_doc, first_row, key_span, 0)
    query_doc = lax.dynamic_slice_in_dim(doc_ids, first_row, row_count, 0)
    query_pos = first_row + jnp.arange(row_count, dtype=jnp.int32)
    key_pos = first_row - REACH * row_count + jnp.arange(key_span, dtype=jnp.int32)
    attended, grad_query, grad_pair = block_grads(
        queries, grad_out, window, query_pos, key_pos, query_doc, key_doc
    )
    partials = grad_pair.reshape(REACH + 1, row_count, 2 * head_dim)[::-1]
    gathered = partials[REACH]
    for offset in range(REACH - 1, -1, -1):
        gathered = from_behind(gathered, "ctx", -1) + partials[offset]
    return (
        attended,
        grad_query,
        gathered[:, :head_dim].astype(jnp.bfloat16),
        gathered[:, head_dim:].astype(jnp.bfloat16),
    )


def solution(mesh):
    return jax.shard_map(
        body,
        mesh=mesh,
        in_specs=(P("ctx", "head"), P("ctx", "head"), P("ctx", "head"), P(), P("ctx", "head")),
        out_specs=(P("ctx", "head"), P("ctx", "head"), P("ctx", "head"), P("ctx", "head")),
        check_vma=False,
    )
```

profile of v0, /device:TPU:381, one launch (start us, length us, event | category | flops | bytes accessed | tf_op | source)
XLA Modules:
  0.0 79.0 jit_solution(6528184009257743200)
XLA Ops:
  0.6 0.9 %constant_dynamic-update-slice_fusion.1 = bf16[256,256]{1,0:T(8,128)(2,1)S(1)} fusion(bf16[256,128]{1,0:T(8,128)(2,1)} %param.6), kind=kLoop, calls=%fused_computation.37 | loop fusion | bytes 131072
  1.5 0.9 %constant_dynamic-update-slice_fusion = bf16[256,256]{1,0:T(8,128)(2,1)S(1)} fusion(bf16[256,256]{1,0:T(8,128)(2,1)S(1)} %constant_dynamic-update-slice_fusion.1, bf16[256,128]{1,0:T(8,128)(2,1)} %param.7), kind=kLoop, calls=%fused_computation.36 | loop fusion | bytes 131072 | tf_op jit(solution)/shard_map/concatenate | solution.py:69
  2.3 5.0 %collective-permute-start = (bf16[256,256]{1,0:T(8,128)(2,1)S(1)}, bf16[256,256]{1,0:T(8,128)(2,1)S(1)}, u32[]{:S(2)}, u32[]{:S(2)}) collective-permute-start(bf16[256,256]{1,0:T(8,128)(2,1)S(1)} %constant_dynamic-update-slice_fusion), channel_id=1, source_target_pairs={{0,4},{4,8},{8,12},{12,16},{16,20},{20,24},{24,28},{28,32},{32,36}... | collective-permute-start | bytes 393224 | tf_op jit(solution)/shard_map/ppermute | solution.py:12
  7.3 1.9 %collective-permute-done = bf16[256,256]{1,0:T(8,128)(2,1)S(1)} collective-permute-done((bf16[256,256]{1,0:T(8,128)(2,1)S(1)}, bf16[256,256]{1,0:T(8,128)(2,1)S(1)}, u32[]{:S(2)}, u32[]{:S(2)}) %collective-permute-start) | collective-permute-done | bytes 131104 | tf_op jit(solution)/shard_map/ppermute | solution.py:12
  9.3 7.7 %collective-permute-start.1 = (bf16[256,256]{1,0:T(8,128)(2,1)S(1)}, bf16[256,256]{1,0:T(8,128)(2,1)S(1)}, u32[]{:S(2)}, u32[]{:S(2)}) collective-permute-start(bf16[256,256]{1,0:T(8,128)(2,1)S(1)} %collective-permute-done), channel_id=1, source_target_pairs={{0,4},{4,8},{8,12},{12,16},{16,20},{20,24},{24,28},{28,32},{32,36}... | collective-permute-start | bytes 393224 | tf_op jit(solution)/shard_map/ppermute | solution.py:12
  16.9 1.2 %copy.12 = bf16[256,1024]{0,1:T(8,128)(2,1)S(1)} copy(bf16[256,1024]{1,0:T(8,128)(2,1)} %param.9) | data formatting | bytes 1048576 | tf_op args[4]
  18.2 1.2 %copy.32 = bf16[256,1024]{0,1:T(8,128)(2,1)S(1)} copy(bf16[256,1024]{1,0:T(8,128)(2,1)} %param.5) | data formatting | bytes 1048576 | tf_op jit(solution)/shard_map/reshape | solution.py:19
  19.4 0.8 dynamic_slice.6
  20.2 0.8 pad_dynamic-slice_fusion
  21.0 0.0 collective-permute-done.1
  21.0 5.5 %collective-permute-start.2 = (bf16[256,256]{1,0:T(8,128)(2,1)S(1)}, bf16[256,256]{1,0:T(8,128)(2,1)S(1)}, u32[]{:S(2)}, u32[]{:S(2)}) collective-permute-start(bf16[256,256]{1,0:T(8,128)(2,1)S(1)} %collective-permute-done.1), channel_id=1, source_target_pairs={{0,4},{4,8},{8,12},{12,16},{16,20},{20,24},{24,28},{28,32},{32,36}... | collective-permute-start | bytes 393224 | tf_op jit(solution)/shard_map/ppermute | solution.py:12
  26.5 0.9 %and_and_fusion = pred[256,1024]{0,1:T(8,128)(4,1)S(1)} fusion(s32[256]{0:T(256)S(1)} %iota_add_fusion.1, s32[256]{0:T(256)S(1)} %dynamic_slice.6, s32[1024]{0:T(1024)S(1)} %get-tuple-element.15, s32[1024]{0:T(1024)S(1)} %get-tuple-element.14, pred[1024]{0:T(1024)(128)(4,1)S(1)} %broadcast_compare_fusion), kind=kLoop, calls=%fused_computation.21 | loop fusion | flops 1048576 | bytes 273408 | tf_op jit(solution)/shard_map/and | solution.py:24
  27.4 1.0 %collective-permute-done.2 = bf16[256,256]{1,0:T(8,128)(2,1)S(1)} collective-permute-done((bf16[256,256]{1,0:T(8,128)(2,1)S(1)}, bf16[256,256]{1,0:T(8,128)(2,1)S(1)}, u32[]{:S(2)}, u32[]{:S(2)}) %collective-permute-start.2) | collective-permute-done | bytes 131104 | tf_op jit(solution)/shard_map/ppermute | solution.py:12
  28.4 0.1 pad_maximum_fusion
  28.6 1.4 %fusion.3 = (f32[8,256]{1,0:T(8,128)S(1)}, f32[1024,256,8]{1,0,2:T(8,128)S(1)}) fusion(pred[256,1024]{0,1:T(8,128)(4,1)S(1)} %and_and_fusion, bf16[256,8,128]{0,2,1:T(8,128)(2,1)S(1)} %bitcast.67, bf16[1024,256]{1,0:T(8,128)(2,1)S(1)} %bitcast.62), kind=kOutput, calls=%fused_computation.7 | convolution fusion | flops 543160320 | bytes 9445376 | tf_op jit(solution)/shard_map/thd,kd->htk/dot_general | solution.py:29
  30.0 2.0 %select_reduce_fusion = f32[8,256]{1,0:T(8,128)S(1)} fusion(f32[1024,256,8]{1,0,2:T(8,128)S(1)} %get-tuple-element.11, f32[8,256]{1,0:T(8,128)S(1)} %get-tuple-element.10, pred[256,1024]{0,1:T(8,128)(4,1)S(1)} %and_and_fusion), kind=kLoop, calls=%fused_computation.5 | loop fusion | flops 10483712 | bytes 8667136 | tf_op jit(solution)/shard_map/reduce_sum | solution.py:34
  32.1 2.3 %multiply_reduce_fusion = (f32[256,8]{0,1:T(8,128)S(1)}, bf16[128,8,256]{2,0,1:T(8,128)(2,1)S(1)}) fusion(bf16[256,1024]{0,1:T(8,128)(2,1)S(1)} %copy.12, f32[1024,256,8]{1,0,2:T(8,128)S(1)} %get-tuple-element.11, f32[8,256]{1,0:T(8,128)S(1)} %log_add_fusion, pred[256,1024]{0,1:T(8,128)(4,1)S(1)} %and_and_fusion, bf16[1024,256]{1,0:T(8,128)(2,1)S(1)} %bitcast.63), kind=kOutput, calls=%fused_computation.20 | convolution fusion | flops 548665344 | bytes 9977856 | tf_op jit(solution)/shard_map/htk,kd->thd/dot_general | solution.py:40
  34.4 2.7 %convolution_bitcast_fusion = f32[1024,128]{0,1:T(8,128)S(1)} fusion(bf16[256,8,128]{0,2,1:T(8,128)(2,1)S(1)} %bitcast.69, f32[1024,256,8]{1,0,2:T(8,128)S(1)} %get-tuple-element.11, f32[8,256]{1,0:T(8,128)S(1)} %log_add_fusion, pred[256,1024]{0,1:T(8,128)(4,1)S(1)} %and_and_fusion), kind=kOutput, calls=%fused_computation.17 | convolution fusion | flops 547356672 | bytes 9707520 | tf_op jit(solution)/shard_map/htk,thd->kd/dot_general | solution.py:56
  37.1 3.1 %fusion.1 = bf16[8,256,1024]{1,2,0:T(8,128)(2,1)S(1)} fusion(f32[1024,256,8]{1,0,2:T(8,128)S(1)} %get-tuple-element.11, f32[8,256]{1,0:T(8,128)S(1)} %bitcast.76, f32[8,256]{1,0:T(8,128)S(1)} %log_add_fusion, pred[256,1024]{0,1:T(8,128)(4,1)S(1)} %and_and_fusion, bf16[256,8,128]{0,2,1:T(8,128)(2,1)S(1)} %bitcast.70, bf16[1024,256]{1,0:T(8,128)(2,1)S(1)} %bitcast.64), kind=kOutput, calls=%fused_computation.2 | convolution fusion | flops 551550976 | bytes 13647872 | tf_op jit(solution)/shard_map/thd,kd->htk/dot_general | solution.py:44
  40.2 0.0 copy-start
  40.2 1.9 %copy-done = bf16[8,256,1024]{1,2,0:T(8,128)(2,1)} copy-done((bf16[8,256,1024]{1,2,0:T(8,128)(2,1)}, bf16[8,256,1024]{1,2,0:T(8,128)(2,1)S(1)}, u32[]{:S(2)}) %copy-start) | copy-done | bytes 4194328
  42.1 1.5 %fusion.5 = f32[1024,128]{0,1:T(8,128)S(1)} fusion(bf16[8,256,1024]{1,2,0:T(8,128)(2,1)S(1)} %fusion.1, bf16[256,8,128]{0,2,1:T(8,128)(2,1)S(1)} %bitcast.68), kind=kOutput, calls=%fused_computation.19 | convolution fusion | flops 537001984 | bytes 5242880 | tf_op jit(solution)/shard_map/htk,thd->kd/dot_general | solution.py:53
  43.6 1.9 %collective-permute-start.3 = (f32[256,256]{0,1:T(8,128)S(1)}, f32[256,256]{0,1:T(8,128)S(1)}, u32[]{:S(2)}, u32[]{:S(2)}) collective-permute-start(f32[256,256]{0,1:T(8,128)S(1)} %fusion.8), channel_id=1, source_target_pairs={{4,0},{8,4},{12,8},{16,12},{20,16},{24,20},{28,24},{32,28},{36,32}... | collective-permute-start | bytes 786440 | tf_op jit(solution)/shard_map/ppermute | solution.py:12
  45.5 9.8 %collective-permute-done.3 = f32[256,256]{0,1:T(8,128)S(1)} collective-permute-done((f32[256,256]{0,1:T(8,128)S(1)}, f32[256,256]{0,1:T(8,128)S(1)}, u32[]{:S(2)}, u32[]{:S(2)}) %collective-permute-start.3) | collective-permute-done | bytes 262176 | tf_op jit(solution)/shard_map/ppermute | solution.py:12
  55.4 1.9 %collective-permute-start.4 = (f32[256,256]{0,1:T(8,128)S(1)}, f32[256,256]{0,1:T(8,128)S(1)}, u32[]{:S(2)}, u32[]{:S(2)}) collective-permute-start(f32[256,256]{0,1:T(8,128)S(1)} %fusion.10), channel_id=1, source_target_pairs={{4,0},{8,4},{12,8},{16,12},{20,16},{24,20},{28,24},{32,28},{36,32}... | collective-permute-start | bytes 786440 | tf_op jit(solution)/shard_map/ppermute | solution.py:12
  57.3 1.0 %copy.19 = bf16[256,1024]{1,0:T(8,128)(2,1)} copy(bf16[256,1024]{0,1:T(8,128)(2,1)S(1)} %bitcast.71) | data formatting | bytes 1048576
  58.3 8.1 %collective-permute-done.4 = f32[256,256]{0,1:T(8,128)S(1)} collective-permute-done((f32[256,256]{0,1:T(8,128)S(1)}, f32[256,256]{0,1:T(8,128)S(1)}, u32[]{:S(2)}, u32[]{:S(2)}) %collective-permute-start.4) | collective-permute-done | bytes 262176 | tf_op jit(solution)/shard_map/ppermute | solution.py:12
  66.4 1.9 %collective-permute-start.5 = (f32[256,256]{0,1:T(8,128)S(1)}, f32[256,256]{0,1:T(8,128)S(1)}, u32[]{:S(2)}, u32[]{:S(2)}) collective-permute-start(f32[256,256]{0,1:T(8,128)S(1)} %fusion.7), channel_id=1, source_target_pairs={{4,0},{8,4},{12,8},{16,12},{20,16},{24,20},{28,24},{32,28},{36,32}... | collective-permute-start | bytes 786440 | tf_op jit(solution)/shard_map/ppermute | solution.py:12
  68.3 2.9 %fusion.4 = bf16[128,8,256]{2,0,1:T(8,128)(2,1)S(1)} fusion(bf16[8,256,1024]{1,2,0:T(8,128)(2,1)} %copy-done, bf16[1024,256]{1,0:T(8,128)(2,1)S(1)} %bitcast.65), kind=kOutput, calls=%fused_computation.15 | convolution fusion | flops 537395200 | bytes 4980736 | tf_op jit(solution)/shard_map/htk,kd->thd/dot_general | solution.py:49
  71.3 1.0 %copy.20 = bf16[256,1024]{1,0:T(8,128)(2,1)} copy(bf16[256,1024]{0,1:T(8,128)(2,1)S(1)} %bitcast.66) | data formatting | bytes 1048576
  72.3 5.1 %collective-permute-done.5 = f32[256,256]{0,1:T(8,128)S(1)} collective-permute-done((f32[256,256]{0,1:T(8,128)S(1)}, f32[256,256]{0,1:T(8,128)S(1)}, u32[]{:S(2)}, u32[]{:S(2)}) %collective-permute-start.5) | collective-permute-done | bytes 262176 | tf_op jit(solution)/shard_map/ppermute | solution.py:12
  77.5 0.7 copy.21
  78.2 0.7 copy.22
  (9 shorter events, 0.2 us)
Async XLA Ops:
  2.3 6.9 %collective-permute-start = (bf16[256,256]{1,0:T(8,128)(2,1)S(1)}, bf16[256,256]{1,0:T(8,128)(2,1)S(1)}, u32[]{:S(2)}, u32[]{:S(2)}) collective-permute-start(bf16[256,256]{1,0:T(8,128)(2,1)S(1)} %constant_dynamic-update-slice_fusion), channel_id=1, source_target_pairs={{0,4},{4,8},{8,12},{12,16},{16,20},{20,24},{24,28},{28,32},{32,36}... | collective-permute-start | bytes 393224 | tf_op jit(solution)/shard_map/ppermute | solution.py:12
  9.3 11.7 %collective-permute-start.1 = (bf16[256,256]{1,0:T(8,128)(2,1)S(1)}, bf16[256,256]{1,0:T(8,128)(2,1)S(1)}, u32[]{:S(2)}, u32[]{:S(2)}) collective-permute-start(bf16[256,256]{1,0:T(8,128)(2,1)S(1)} %collective-permute-done), channel_id=1, source_target_pairs={{0,4},{4,8},{8,12},{12,16},{16,20},{20,24},{24,28},{28,32},{32,36}... | collective-permute-start | bytes 393224 | tf_op jit(solution)/shard_map/ppermute | solution.py:12
  21.0 7.5 %collective-permute-start.2 = (bf16[256,256]{1,0:T(8,128)(2,1)S(1)}, bf16[256,256]{1,0:T(8,128)(2,1)S(1)}, u32[]{:S(2)}, u32[]{:S(2)}) collective-permute-start(bf16[256,256]{1,0:T(8,128)(2,1)S(1)} %collective-permute-done.1), channel_id=1, source_target_pairs={{0,4},{4,8},{8,12},{12,16},{16,20},{20,24},{24,28},{28,32},{32,36}... | collective-permute-start | bytes 393224 | tf_op jit(solution)/shard_map/ppermute | solution.py:12
  40.2 1.9 %copy-start = (bf16[8,256,1024]{1,2,0:T(8,128)(2,1)}, bf16[8,256,1024]{1,2,0:T(8,128)(2,1)S(1)}, u32[]{:S(2)}) copy-start(bf16[8,256,1024]{1,2,0:T(8,128)(2,1)S(1)} %fusion.1) | copy-start | bytes 12582916
  43.6 11.7 %collective-permute-start.3 = (f32[256,256]{0,1:T(8,128)S(1)}, f32[256,256]{0,1:T(8,128)S(1)}, u32[]{:S(2)}, u32[]{:S(2)}) collective-permute-start(f32[256,256]{0,1:T(8,128)S(1)} %fusion.8), channel_id=1, source_target_pairs={{4,0},{8,4},{12,8},{16,12},{20,16},{24,20},{28,24},{32,28},{36,32}... | collective-permute-start | bytes 786440 | tf_op jit(solution)/shard_map/ppermute | solution.py:12
  55.4 11.0 %collective-permute-start.4 = (f32[256,256]{0,1:T(8,128)S(1)}, f32[256,256]{0,1:T(8,128)S(1)}, u32[]{:S(2)}, u32[]{:S(2)}) collective-permute-start(f32[256,256]{0,1:T(8,128)S(1)} %fusion.10), channel_id=1, source_target_pairs={{4,0},{8,4},{12,8},{16,12},{20,16},{24,20},{28,24},{32,28},{36,32}... | collective-permute-start | bytes 786440 | tf_op jit(solution)/shard_map/ppermute | solution.py:12
  66.4 11.0 %collective-permute-start.5 = (f32[256,256]{0,1:T(8,128)S(1)}, f32[256,256]{0,1:T(8,128)S(1)}, u32[]{:S(2)}, u32[]{:S(2)}) collective-permute-start(f32[256,256]{0,1:T(8,128)S(1)} %fusion.7), channel_id=1, source_target_pairs={{4,0},{8,4},{12,8},{16,12},{20,16},{24,20},{28,24},{32,28},{36,32}... | collective-permute-start | bytes 786440 | tf_op jit(solution)/shard_map/ppermute | solution.py:12
where the time goes:
time: 79.5 us; the launch traced here: 79 us
  waiting for transfers between devices  25.9 us (33%)
  starting transfers between devices  23.9 us (30%)
  matrix products  13.9 us (17%)
  local copies, waits for them, and re-layouts  10.4 us (13%)
  other arithmetic  3.96 us (5%)
  between operations  0.83 us (1%)
    ppermute x6, waiting for transfers between devices, from_behind(): return lax.ppermute(value, axis, pairs)  25.9 us
    ppermute x6, starting transfers between devices, from_behind(): return lax.ppermute(value, axis, pairs)  23.9 us
    unnamed x8, local copies, waits for them, and re-layouts  7.5 us
    dot_general x1, matrix products, block_grads(): jnp.einsum('thd,kd->htk', grad_heads, value_part, preferred_element_type=...  3.08 us
    dot_general x1, matrix products, block_grads(): jnp.einsum('htk,kd->thd', dscore, key_part, preferred_element_type=jnp.fl...  2.94 us
    dot_general x1, matrix products, block_grads(): jnp.einsum('htk,thd->kd', weights, grad_heads, preferred_element_type=jnp...  2.68 us
    dot_general x1, matrix products, block_grads(): jnp.einsum('htk,kd->thd', weights, value_part, preferred_element_type=jnp...  2.33 us
    reduce_sum x1, other arithmetic, block_grads(): jnp.sum(jnp.where(allowed[None], jnp.exp(scores - row_max), 0.0), axis=-1...  2.04 us
  transfers between devices with their start and end apart: 6, of which 5 were waited for; matrix products, arithmetic and copies ran while one was open for 13% of the time, Pallas kernels for 0%

commit v1 on v0

v1 whole, which is shorter than its diff:
```python
import functools
import math

import jax
import jax.numpy as jnp
from jax import lax
from jax.experimental import pallas as pl
from jax.experimental.pallas import tpu as pltpu
from jax.sharding import PartitionSpec as P

REACH = 3
OWN = REACH
F32 = jnp.float32
BF16 = jnp.bfloat16
MESH = pl.DeviceIdType.MESH
NT = (((1,), (1,)), ((), ()))
NN = (((1,), (0,)), ((), ()))


def dot(a, b, dims=NN):
    return lax.dot_general(a, b, dims, preferred_element_type=F32)


def fill_bias(doc, bias):
    rows = doc.shape[2]
    total = doc.shape[1] * rows
    query_doc = jnp.concatenate([doc[OWN, i : i + 1, :] for i in range(doc.shape[1])], axis=1)
    query_doc = jnp.broadcast_to(query_doc, (rows, total))
    for part in range(doc.shape[1]):

        def column(slot):
            line = jnp.broadcast_to(doc[slot, part : part + 1, :], (rows, rows))
            return jnp.broadcast_to(jnp.transpose(line)[:, 0:1], (rows, total))

        key_at = lax.broadcasted_iota(jnp.int32, (rows, total), 0) + part * rows
        query_at = lax.broadcasted_iota(jnp.int32, (rows, total), 1)
        folded = jnp.where(key_at <= query_at, column(OWN), column(0))
        for block, key_doc in ((0, folded), (1, column(1)), (2, column(2))):
            bias[block, pl.ds(part * rows, rows), :] = jnp.where(key_doc == query_doc, 0.0, -1e30)


def kernel(
    n,
    q_hbm,
    g_hbm,
    k_hbm,
    v_hbm,
    doc_hbm,
    att_ref,
    dq_ref,
    dk_ref,
    dv_ref,
    q,
    g,
    keys,
    values,
    doc,
    bias,
    weights,
    dscores,
    own_grad,
    out_grad,
    in_grad,
    local_sem,
    kv_send,
    kv_recv,
    grad_send,
    grad_recv,
):
    heads, rows, dim = q.shape
    scale = 1.0 / math.sqrt(dim)
    me = lax.axis_index("ctx")

    local = []
    for slot in range(REACH + 1):
        block = lax.rem(me + n - REACH + slot, n)
        local.append(pltpu.make_async_copy(doc_hbm.at[block], doc.at[slot], local_sem.at[0, slot]))
    local.append(pltpu.make_async_copy(k_hbm, keys.at[OWN], local_sem.at[0, 4]))
    local.append(pltpu.make_async_copy(v_hbm, values.at[OWN], local_sem.at[0, 5]))
    for h in range(heads):
        columns = pl.ds(h * dim, dim)
        local.append(pltpu.make_async_copy(q_hbm.at[:, columns], q.at[h], local_sem.at[1, h]))
        local.append(pltpu.make_async_copy(g_hbm.at[:, columns], g.at[h], local_sem.at[2, h]))
    for copy in local:
        copy.start()

    barrier = pltpu.get_barrier_semaphore()
    for d in range(1, REACH + 1):
        for other in (lax.rem(me + d, n), lax.rem(me + n - d, n)):
            pl.semaphore_signal(barrier, inc=1, device_id={"ctx": other}, device_id_type=MESH)
    pl.semaphore_wait(barrier, 2 * REACH)

    moves = []
    for which, (source, target) in enumerate(((k_hbm, keys), (v_hbm, values))):
        for d in range(1, REACH + 1):
            moves.append(
                pltpu.make_async_remote_copy(
                    src_ref=source,
                    dst_ref=target.at[REACH - d],
                    send_sem=kv_send.at[which, d - 1],
                    recv_sem=kv_recv.at[which, d - 1],
                    device_id={"ctx": lax.rem(me + d, n)},
                    device_id_type=MESH,
                )
            )
    for move in moves:
        move.start()

    for copy in local[: REACH + 1]:
        copy.wait()
    fill_bias(doc, bias)
    for copy in local[REACH + 1 :]:
        copy.wait()
    for move in moves:
        move.wait()

    exponent = math.log2(math.e) * scale
    key_at = lax.broadcasted_iota(jnp.int32, (rows, rows), 0)
    query_at = lax.broadcasted_iota(jnp.int32, (rows, rows), 1)
    own = key_at <= query_at
    for h in range(heads):
        columns = pl.ds(h * rows, rows)
        s = [dot(keys[j], q[h], NT) for j in range(REACH + 1)]
        s = [jnp.where(own, s[OWN], s[0]) + bias[0], s[1] + bias[1], s[2] + bias[2]]
        top = jnp.maximum(jnp.maximum(s[0], s[1]), s[2]).max(axis=0, keepdims=True)
        e = [jnp.exp2((x - top) * exponent) for x in s]
        inverse = 1.0 / (e[0] + e[1] + e[2]).sum(axis=0, keepdims=True)
        d = [dot(values[j], g[h], NT) for j in range(REACH + 1)]
        d = [jnp.where(own, d[OWN], d[0]), d[1], d[2]]
        w = [x * inverse for x in e]
        delta = (w[0] * d[0] + w[1] * d[1] + w[2] * d[2]).sum(axis=0, keepdims=True)
        ds = [x * (y - delta) for x, y in zip(w, d)]
        for ref, v in ((weights, w), (dscores, ds)):
            ref[0, :, columns] = jnp.where(own, 0.0, v[0]).astype(BF16)
            ref[OWN, :, columns] = jnp.where(own, v[0], 0.0).astype(BF16)
            ref[1, :, columns] = v[1].astype(BF16)
            ref[2, :, columns] = v[2].astype(BF16)

    sends = []
    for j in range(REACH + 1):
        dv = dot(weights[j], g[...].reshape(heads * rows, dim))
        dk = dot(dscores[j], q[...].reshape(heads * rows, dim)) * scale
        if j == OWN:
            own_grad[0] = dk
            own_grad[1] = dv
            continue
        d = REACH - j
        out_grad[d - 1, 0] = dk.astype(BF16)
        out_grad[d - 1, 1] = dv.astype(BF16)
        sends.append(
            pltpu.make_async_remote_copy(
                src_ref=out_grad.at[d - 1],
                dst_ref=in_grad.at[d - 1],
                send_sem=grad_send.at[d - 1],
                recv_sem=grad_recv.at[d - 1],
                device_id={"ctx": lax.rem(me + n - d, n)},
                device_id_type=MESH,
            )
        )
        sends[-1].start()

    keys_t = [jnp.transpose(keys[j]) for j in range(REACH + 1)]
    values_t = [jnp.transpose(values[j]) for j in range(REACH + 1)]
    for h in range(heads):
        columns = pl.ds(h * rows, rows)
        att = sum(dot(values_t[j], weights[j, :, columns]) for j in range(REACH + 1))
        att_ref[:, pl.ds(h * dim, dim)] = jnp.transpose(att).astype(BF16)
        dq = sum(dot(keys_t[j], dscores[j, :, columns]) for j in range(REACH + 1)) * scale
        dq_ref[:, pl.ds(h * dim, dim)] = jnp.transpose(dq).astype(BF16)

    for send in sends:
        send.wait()
    for which, ref in ((0, dk_ref), (1, dv_ref)):
        total = own_grad[which]
        for d in range(REACH):
            total = total + in_grad[d, which].astype(F32)
        ref[...] = total.astype(BF16)


def hand_over(*refs):
    count = (len(refs) - 1) // 2
    sem = refs[-1]
    copies = [
        pltpu.make_async_copy(refs[i], refs[count + i], sem.at[i]) for i in range(count)
    ]
    for copy in copies:
        copy.start()
    for copy in copies:
        copy.wait()


def body(n, queries, key_vectors, value_vectors, doc_ids, grad_out):
    rows, width = queries.shape
    dim = key_vectors.shape[1]
    heads = width // dim
    lanes = 128
    doc = doc_ids.reshape(n, rows // lanes, lanes)
    hbm = pl.BlockSpec(memory_space=pltpu.HBM)
    vmem = pl.BlockSpec(memory_space=pltpu.VMEM)
    shapes = [
        jax.ShapeDtypeStruct((rows, width), BF16),
        jax.ShapeDtypeStruct((rows, width), BF16),
        jax.ShapeDtypeStruct((rows, dim), BF16),
        jax.ShapeDtypeStruct((rows, dim), BF16),
    ]
    blocks = REACH + 1
    results = pl.pallas_call(
        functools.partial(kernel, n),
        out_shape=shapes,
        in_specs=[hbm] * 5,
        out_specs=[vmem] * 4,
        scratch_shapes=[
            pltpu.VMEM((heads, rows, dim), BF16),
            pltpu.VMEM((heads, rows, dim), BF16),
            pltpu.VMEM((blocks, rows, dim), BF16),
            pltpu.VMEM((blocks, rows, dim), BF16),
            pltpu.VMEM((blocks, rows // lanes, lanes), jnp.int32),
            pltpu.VMEM((REACH, rows, rows), F32),
            pltpu.VMEM((blocks, rows, heads * rows), BF16),
            pltpu.VMEM((blocks, rows, heads * rows), BF16),
            pltpu.VMEM((2, rows, dim), F32),
            pltpu.VMEM((REACH, 2, rows, dim), BF16),
            pltpu.VMEM((REACH, 2, rows, dim), BF16),
            pltpu.SemaphoreType.DMA((3, 8)),
            pltpu.SemaphoreType.DMA((2, REACH)),
            pltpu.SemaphoreType.DMA((2, REACH)),
            pltpu.SemaphoreType.DMA((REACH,)),
            pltpu.SemaphoreType.DMA((REACH,)),
        ],
        compiler_params=pltpu.CompilerParams(
            collective_id=0, has_side_effects=True, vmem_limit_bytes=40 << 20
        ),
    )(queries, grad_out, key_vectors, value_vectors, doc)
    return pl.pallas_call(
        hand_over,
        out_shape=shapes,
        in_specs=[vmem] * 4,
        out_specs=[hbm] * 4,
        scratch_shapes=[pltpu.SemaphoreType.DMA((4,))],
        compiler_params=pltpu.CompilerParams(vmem_limit_bytes=8 << 20),
    )(*results)


def solution(mesh):
    return jax.shard_map(
        functools.partial(body, mesh.shape["ctx"]),
        mesh=mesh,
        in_specs=(P("ctx", "head"), P("ctx", "head"), P("ctx", "head"), P(), P("ctx", "head")),
        out_specs=(P("ctx", "head"), P("ctx", "head"), P("ctx", "head"), P("ctx", "head")),
        check_vma=False,
    )
```

time: 79.5 us -> 49.8 us (0.63)
  the two profiles are of different devices: /device:TPU:381 before, /device:TPU:1 now
where the time goes in v1:
time: 49.8 us; the launch traced here: 49.4 us
  Pallas kernels  44 us (88%)
  local copies, waits for them, and re-layouts  4.7 us (9%)
  between operations  0.65 us (1%)
    pallas_call x1, Pallas kernels, body(): pl.pallas_call(functools.partial(kernel, n), out_shape=shapes, in_specs=[...  43 us
    unnamed x10, local copies, waits for them, and re-layouts  4.7 us
    pallas_call x1, Pallas kernels, body(): pl.pallas_call(hand_over, out_shape=shapes, in_specs=[vmem] * 4, out_spec...  1.03 us

profile of v1, /device:TPU:1, one launch (start us, length us, event | category | flops | bytes accessed | tf_op | source)
XLA Modules:
  0.0 49.4 jit_solution(10024941578908013019)
XLA Ops:
  0.6 0.0 copy-start
  0.6 1.0 %copy-done = bf16[256,1024]{1,0:T(8,128)(2,1)S(1)} copy-done((bf16[256,1024]{1,0:T(8,128)(2,1)S(1)}, bf16[256,1024]{1,0:T(8,128)(2,1)}, u32[]{:S(2)}) %copy-start) | copy-done | bytes 524312
  1.7 0.0 copy-start.1
  1.7 1.0 %copy-done.1 = bf16[256,1024]{1,0:T(8,128)(2,1)S(1)} copy-done((bf16[256,1024]{1,0:T(8,128)(2,1)S(1)}, bf16[256,1024]{1,0:T(8,128)(2,1)}, u32[]{:S(2)}) %copy-start.1) | copy-done | bytes 524312
  2.7 0.0 copy-start.2
  2.7 0.9 %copy-done.2 = s32[65536]{0:T(1024)S(1)} copy-done((s32[65536]{0:T(1024)S(1)}, s32[65536]{0:T(1024)}, u32[]{:S(2)}) %copy-start.2) | copy-done | bytes 262168
  3.7 0.0 copy-start.3
  3.7 0.8 %copy-done.3 = bf16[256,128]{1,0:T(8,128)(2,1)S(1)} copy-done((bf16[256,128]{1,0:T(8,128)(2,1)S(1)}, bf16[256,128]{1,0:T(8,128)(2,1)}, u32[]{:S(2)}) %copy-start.3) | copy-done | bytes 65560
  4.5 0.0 copy-start.4
  4.5 0.8 %copy-done.4 = bf16[256,128]{1,0:T(8,128)(2,1)S(1)} copy-done((bf16[256,128]{1,0:T(8,128)(2,1)S(1)}, bf16[256,128]{1,0:T(8,128)(2,1)}, u32[]{:S(2)}) %copy-start.4) | copy-done | bytes 65560
  5.3 43.0 %shard_map.84 = (bf16[256,1024]{1,0:T(8,128)(2,1)S(1)}, bf16[256,1024]{1,0:T(8,128)(2,1)S(1)}, bf16[256,128]{1,0:T(8,128)(2,1)S(1)}, bf16[256,128]{1,0:T(8,128)(2,1)S(1)}) custom-call(bf16[256,1024]{1,0:T(8,128)(2,1)S(1)} %copy-done, bf16[256,1024]{1,0:T(8,128)(2,1)S(1)} %copy-done.1, bf16[256,128]{1,0:T(8,128)(2,1)S(1)} %copy-done.3, ...), custom_call_target="tpu_custom_call" | custom-call | tf_op jit(solution)/shard_map/pallas_call | solution.py:207
  48.4 1.0 %shard_map.85 = (bf16[256,1024]{1,0:T(8,128)(2,1)}, bf16[256,1024]{1,0:T(8,128)(2,1)}, bf16[256,128]{1,0:T(8,128)(2,1)}, bf16[256,128]{1,0:T(8,128)(2,1)}) custom-call(bf16[256,1024]{1,0:T(8,128)(2,1)S(1)} %get-tuple-element.8.refs_0_, bf16[256,1024]{1,0:T(8,128)(2,1)S(1)} %get-tuple-element.9.refs_1_, bf16[256,128]{1,0:T(8,128)(2,1)S(1)} %get-tuple-element.10.refs_2_, ...), custom_call_target="tpu_custom_call" | custom-call | tf_op jit(solution)/shard_map/pallas_call | solution.py:234
Async XLA Ops:
  0.6 1.0 %copy-start = (bf16[256,1024]{1,0:T(8,128)(2,1)S(1)}, bf16[256,1024]{1,0:T(8,128)(2,1)}, u32[]{:S(2)}) copy-start(bf16[256,1024]{1,0:T(8,128)(2,1)} %q_hbm.1) | copy-start | bytes 1572868
  1.7 1.0 %copy-start.1 = (bf16[256,1024]{1,0:T(8,128)(2,1)S(1)}, bf16[256,1024]{1,0:T(8,128)(2,1)}, u32[]{:S(2)}) copy-start(bf16[256,1024]{1,0:T(8,128)(2,1)} %g_hbm.1) | copy-start | bytes 1572868
  2.7 0.9 %copy-start.2 = (s32[65536]{0:T(1024)S(1)}, s32[65536]{0:T(1024)}, u32[]{:S(2)}) copy-start(s32[65536]{0:T(1024)} %param.8) | copy-start | bytes 786436
  3.7 0.8 %copy-start.3 = (bf16[256,128]{1,0:T(8,128)(2,1)S(1)}, bf16[256,128]{1,0:T(8,128)(2,1)}, u32[]{:S(2)}) copy-start(bf16[256,128]{1,0:T(8,128)(2,1)} %k_hbm.1) | copy-start | bytes 196612
  4.5 0.8 %copy-start.4 = (bf16[256,128]{1,0:T(8,128)(2,1)S(1)}, bf16[256,128]{1,0:T(8,128)(2,1)}, u32[]{:S(2)}) copy-start(bf16[256,128]{1,0:T(8,128)(2,1)} %v_hbm.1) | copy-start | bytes 196612

commit v2 on v1

v2 whole, which is shorter than its diff:
```python
import functools
import math

import jax
import jax.numpy as jnp
from jax import lax
from jax.experimental import pallas as pl
from jax.experimental.pallas import tpu as pltpu
from jax.sharding import PartitionSpec as P

REACH = 3
OWN = REACH
F32 = jnp.float32
BF16 = jnp.bfloat16
MESH = pl.DeviceIdType.MESH
NT = (((1,), (1,)), ((), ()))
NN = (((1,), (0,)), ((), ()))


def dot(a, b, dims=NN):
    return lax.dot_general(a, b, dims, preferred_element_type=F32)


def fill_bias(doc, bias):
    rows = doc.shape[2]
    total = doc.shape[1] * rows
    query_doc = jnp.concatenate([doc[OWN, i : i + 1, :] for i in range(doc.shape[1])], axis=1)
    query_doc = jnp.broadcast_to(query_doc, (rows, total))
    for part in range(doc.shape[1]):
        for slot in range(REACH + 1):
            line = jnp.broadcast_to(doc[slot, part : part + 1, :], (rows, rows))
            allowed = jnp.broadcast_to(jnp.transpose(line)[:, 0:1], (rows, total)) == query_doc
            if slot == OWN:
                key_at = lax.broadcasted_iota(jnp.int32, (rows, total), 0) + part * rows
                query_at = lax.broadcasted_iota(jnp.int32, (rows, total), 1)
                allowed = allowed & (key_at <= query_at)
            bias[slot, pl.ds(part * rows, rows), :] = jnp.where(allowed, 0.0, -1e30)


def kernel(
    n,
    q_hbm,
    g_hbm,
    k_hbm,
    v_hbm,
    doc_hbm,
    att_ref,
    dq_ref,
    dk_ref,
    dv_ref,
    q,
    g,
    keys,
    values,
    doc,
    bias,
    stats,
    factors,
    raw,
    slopes,
    weights,
    dscores,
    own_grad,
    out_grad,
    in_grad,
    local_sem,
    kv_send,
    kv_recv,
    grad_send,
    grad_recv,
):
    heads, rows, dim = q.shape
    scale = 1.0 / math.sqrt(dim)
    exponent = math.log2(math.e) * scale
    me = lax.axis_index("ctx")
    reach = range(1, REACH + 1)

    local = []
    for slot in range(REACH + 1):
        block = lax.rem(me + n - REACH + slot, n)
        local.append(pltpu.make_async_copy(doc_hbm.at[block], doc.at[slot], local_sem.at[0, slot]))
    local.append(pltpu.make_async_copy(k_hbm, keys.at[OWN], local_sem.at[0, 4]))
    local.append(pltpu.make_async_copy(v_hbm, values.at[OWN], local_sem.at[0, 5]))
    for h in range(heads):
        columns = pl.ds(h * dim, dim)
        local.append(pltpu.make_async_copy(q_hbm.at[:, columns], q.at[h], local_sem.at[1, h]))
        local.append(pltpu.make_async_copy(g_hbm.at[:, columns], g.at[h], local_sem.at[2, h]))
    for copy in local:
        copy.start()

    barrier = pltpu.get_barrier_semaphore()

    def greet(there, other):
        @pl.when(there)
        def _():
            pl.semaphore_signal(barrier, inc=1, device_id={"ctx": other}, device_id_type=MESH)

    for d in reach:

        @pl.when(me < d)
        def _():
            keys[REACH - d] = jnp.zeros(keys.shape[1:], BF16)
            values[REACH - d] = jnp.zeros(values.shape[1:], BF16)

    for d in reach:
        greet(me + d < n, me + d)
        greet(me >= d, me - d)
    for missing in range(REACH + 1):
        if missing:
            here = (me == REACH - missing) | (me == n - 1 - REACH + missing)
        else:
            here = (me >= REACH) & (me < n - REACH)

        @pl.when(here)
        def _():
            pl.semaphore_wait(barrier, 2 * REACH - missing)

    def kv_moves(d):
        return [
            pltpu.make_async_remote_copy(
                src_ref=source,
                dst_ref=target.at[REACH - d],
                send_sem=kv_send.at[which, d - 1],
                recv_sem=kv_recv.at[which, d - 1],
                device_id={"ctx": me + d},
                device_id_type=MESH,
            )
            for which, (source, target) in enumerate(((k_hbm, keys), (v_hbm, values)))
        ]

    def grad_move(d):
        return pltpu.make_async_remote_copy(
            src_ref=out_grad.at[d - 1],
            dst_ref=in_grad.at[d - 1],
            send_sem=grad_send.at[d - 1],
            recv_sem=grad_recv.at[d - 1],
            device_id={"ctx": me - d},
            device_id_type=MESH,
        )

    for d in reach:

        @pl.when(me + d < n)
        def _():
            for move in kv_moves(d):
                move.start()

    for copy in local[: REACH + 1]:
        copy.wait()
    fill_bias(doc, bias)
    stats[0] = jnp.full(stats.shape[1:], -1e30, F32)
    stats[1] = jnp.zeros(stats.shape[1:], F32)
    stats[2] = jnp.zeros(stats.shape[1:], F32)
    for copy in local[REACH + 1 :]:
        copy.wait()

    def first_pass(j):
        for h in range(heads):
            columns = pl.ds(h * rows, rows)
            s = dot(keys[j], q[h], NT) + bias[j]
            top = s.max(axis=0, keepdims=True)
            e = jnp.exp2((s - top) * exponent)
            slope = dot(values[j], g[h], NT)
            stats[0, j, h : h + 1, :] = top
            stats[1, j, h : h + 1, :] = e.sum(axis=0, keepdims=True)
            stats[2, j, h : h + 1, :] = (e * slope).sum(axis=0, keepdims=True)
            raw[j, :, columns] = e
            slopes[j, :, columns] = slope

    first_pass(OWN)
    for d in reach:

        @pl.when(me >= d)
        def _():
            for move in kv_moves(d):
                move.wait_recv()
            first_pass(REACH - d)

    tops = [stats[0, j] for j in range(REACH + 1)]
    top = jnp.maximum(jnp.maximum(tops[0], tops[1]), jnp.maximum(tops[2], tops[3]))
    grown = [jnp.exp2((x - top) * exponent) for x in tops]
    inverse = 1.0 / sum(x * stats[1, j] for j, x in enumerate(grown))
    delta = sum(x * stats[2, j] for j, x in enumerate(grown)) * inverse
    for j in range(REACH + 1):
        factors[j] = grown[j] * inverse
    factors[REACH + 1] = delta

    def second_pass(j):
        for h in range(heads):
            columns = pl.ds(h * rows, rows)
            w = raw[j, :, columns] * factors[j, h : h + 1, :]
            weights[j, :, columns] = w.astype(BF16)
            ds = w * (slopes[j, :, columns] - factors[REACH + 1, h : h + 1, :])
            dscores[j, :, columns] = ds.astype(BF16)
        dv = dot(weights[j], g[...].reshape(heads * rows, dim))
        dk = dot(dscores[j], q[...].reshape(heads * rows, dim)) * scale
        return dk, dv

    for d in reach:
        j = REACH - d

        @pl.when(me >= d)
        def _():
            dk, dv = second_pass(j)
            out_grad[d - 1, 0] = dk.astype(BF16)
            out_grad[d - 1, 1] = dv.astype(BF16)
            grad_move(d).start()

        @pl.when(me < d)
        def _():
            weights[j] = jnp.zeros(weights.shape[1:], BF16)
            dscores[j] = jnp.zeros(dscores.shape[1:], BF16)

    dk, dv = second_pass(OWN)
    own_grad[0] = dk
    own_grad[1] = dv

    keys_t = [jnp.transpose(keys[j]) for j in range(REACH + 1)]
    values_t = [jnp.transpose(values[j]) for j in range(REACH + 1)]
    for h in range(heads):
        columns = pl.ds(h * rows, rows)
        att = sum(dot(values_t[j], weights[j, :, columns]) for j in range(REACH + 1))
        att_ref[:, pl.ds(h * dim, dim)] = jnp.transpose(att).astype(BF16)
        dq = sum(dot(keys_t[j], dscores[j, :, columns]) for j in range(REACH + 1)) * scale
        dq_ref[:, pl.ds(h * dim, dim)] = jnp.transpose(dq).astype(BF16)

    for d in reach:

        @pl.when(me + d < n)
        def _():
            for move in kv_moves(d):
                move.wait_send()
            grad_move(d).wait_recv()
            for which in range(2):
                own_grad[which] += in_grad[d - 1, which].astype(F32)

        @pl.when(me >= d)
        def _():
            grad_move(d).wait_send()

    dk_ref[...] = own_grad[0].astype(BF16)
    dv_ref[...] = own_grad[1].astype(BF16)


def hand_over(*refs):
    count = (len(refs) - 1) // 2
    sem = refs[-1]
    copies = [
        pltpu.make_async_copy(refs[i], refs[count + i], sem.at[i]) for i in range(count)
    ]
    for copy in copies:
        copy.start()
    for copy in copies:
        copy.wait()


def body(n, queries, key_vectors, value_vectors, doc_ids, grad_out):
    rows, width = queries.shape
    dim = key_vectors.shape[1]
    heads = width // dim
    lanes = 128
    doc = doc_ids.reshape(n, rows // lanes, lanes)
    hbm = pl.BlockSpec(memory_space=pltpu.HBM)
    vmem = pl.BlockSpec(memory_space=pltpu.VMEM)
    shapes = [
        jax.ShapeDtypeStruct((rows, width), BF16),
        jax.ShapeDtypeStruct((rows, width), BF16),
        jax.ShapeDtypeStruct((rows, dim), BF16),
        jax.ShapeDtypeStruct((rows, dim), BF16),
    ]
    blocks = REACH + 1
    results = pl.pallas_call(
        functools.partial(kernel, n),
        out_shape=shapes,
        in_specs=[hbm] * 5,
        out_specs=[vmem] * 4,
        scratch_shapes=[
            pltpu.VMEM((heads, rows, dim), BF16),
            pltpu.VMEM((heads, rows, dim), BF16),
            pltpu.VMEM((blocks, rows, dim), BF16),
            pltpu.VMEM((blocks, rows, dim), BF16),
            pltpu.VMEM((blocks, rows // lanes, lanes), jnp.int32),
            pltpu.VMEM((blocks, rows, rows), F32),
            pltpu.VMEM((3, blocks, heads, rows), F32),
            pltpu.VMEM((blocks + 1, heads, rows), F32),
            pltpu.VMEM((blocks, rows, heads * rows), F32),
            pltpu.VMEM((blocks, rows, heads * rows), F32),
            pltpu.VMEM((blocks, rows, heads * rows), BF16),
            pltpu.VMEM((blocks, rows, heads * rows), BF16),
            pltpu.VMEM((2, rows, dim), F32),
            pltpu.VMEM((REACH, 2, rows, dim), BF16),
            pltpu.VMEM((REACH, 2, rows, dim), BF16),
            pltpu.SemaphoreType.DMA((3, 8)),
            pltpu.SemaphoreType.DMA((2, REACH)),
            pltpu.SemaphoreType.DMA((2, REACH)),
            pltpu.SemaphoreType.DMA((REACH,)),
            pltpu.SemaphoreType.DMA((REACH,)),
        ],
        compiler_params=pltpu.CompilerParams(
            collective_id=0, has_side_effects=True, vmem_limit_bytes=48 << 20
        ),
    )(*(pltpu.with_memory_space_constraint(x, pltpu.HBM) for x in (queries, grad_out, key_vectors, value_vectors, doc)))
    return pl.pallas_call(
        hand_over,
        out_shape=shapes,
        in_specs=[vmem] * 4,
        out_specs=[hbm] * 4,
        scratch_shapes=[pltpu.SemaphoreType.DMA((4,))],
        compiler_params=pltpu.CompilerParams(vmem_limit_bytes=8 << 20),
    )(*results)


def solution(mesh):
    return jax.shard_map(
        functools.partial(body, mesh.shape["ctx"]),
        mesh=mesh,
        in_specs=(P("ctx", "head"), P("ctx", "head"), P("ctx", "head"), P(), P("ctx", "head")),
        out_specs=(P("ctx", "head"), P("ctx", "head"), P("ctx", "head"), P("ctx", "head")),
        check_vma=False,
    )
```

time: 49.8 us -> 35.8 us (0.72)
  Pallas kernels: 44 us -> 34.9 us
  local copies, waits for them, and re-layouts: 4.7 us -> 0 us
    pallas_call x1, Pallas kernels: 43 us -> 33.8 us  [body(): pl.pallas_call(functools.partial(kernel, n), out_shape=shapes, in_specs=[...]
    unnamed x10 -> x0, local copies, waits for them, and re-layouts: 4.7 us -> none
where the time goes in v2:
time: 35.8 us; the launch traced here: 35.5 us
  Pallas kernels  34.9 us (97%)
  between operations  0.64 us (2%)
    pallas_call x1, Pallas kernels, body(): pl.pallas_call(functools.partial(kernel, n), out_shape=shapes, in_specs=[...  33.8 us
    pallas_call x1, Pallas kernels, body(): pl.pallas_call(hand_over, out_shape=shapes, in_specs=[vmem] * 4, out_spec...  1.03 us

profile of v2, /device:TPU:1, one launch (start us, length us, event | category | flops | bytes accessed | tf_op | source)
XLA Modules:
  0.0 35.5 jit_solution(14370303736791984800)
XLA Ops:
  0.6 33.8 %shard_map.84 = (bf16[256,1024]{1,0:T(8,128)(2,1)S(1)}, bf16[256,1024]{1,0:T(8,128)(2,1)S(1)}, bf16[256,128]{1,0:T(8,128)(2,1)S(1)}, bf16[256,128]{1,0:T(8,128)(2,1)S(1)}) custom-call(bf16[256,1024]{1,0:T(8,128)(2,1)} %q_hbm.1, bf16[256,1024]{1,0:T(8,128)(2,1)} %g_hbm.1, bf16[256,128]{1,0:T(8,128)(2,1)} %k_hbm.1, bf16[256,128]{1,0:T(8,128)(2,1)} %v_hbm.1, ...), custom_call_target="tpu_custom_call" | custom-call | tf_op jit(solution)/shard_map/pallas_call | solution.py:272
  34.5 1.0 %shard_map.85 = (bf16[256,1024]{1,0:T(8,128)(2,1)}, bf16[256,1024]{1,0:T(8,128)(2,1)}, bf16[256,128]{1,0:T(8,128)(2,1)}, bf16[256,128]{1,0:T(8,128)(2,1)}) custom-call(bf16[256,1024]{1,0:T(8,128)(2,1)S(1)} %get-tuple-element.8.refs_0_, bf16[256,1024]{1,0:T(8,128)(2,1)S(1)} %get-tuple-element.9.refs_1_, bf16[256,128]{1,0:T(8,128)(2,1)S(1)} %get-tuple-element.10.refs_2_, ...), custom_call_target="tpu_custom_call" | custom-call | tf_op jit(solution)/shard_map/pallas_call | solution.py:303

commit v3 on v2

--- a/solution.py
+++ b/solution.py
@@ -103,17 +103,13 @@
             values[REACH - d] = jnp.zeros(values.shape[1:], BF16)
 
     for d in reach:
-        greet(me + d < n, me + d)
         greet(me >= d, me - d)
-    for missing in range(REACH + 1):
-        if missing:
-            here = (me == REACH - missing) | (me == n - 1 - REACH + missing)
-        else:
-            here = (me >= REACH) & (me < n - REACH)
+    for missing in range(REACH):
+        here = me == n - 1 - REACH + missing if missing else me < n - REACH
 
         @pl.when(here)
         def _():
-            pl.semaphore_wait(barrier, 2 * REACH - missing)
+            pl.semaphore_wait(barrier, REACH - missing)
 
     def kv_moves(d):
         return [

time: 35.8 us -> 29.9 us (0.84)
  Pallas kernels: 34.9 us -> 29 us
    pallas_call x1, Pallas kernels: 33.8 us -> 28 us  [body(): pl.pallas_call(functools.partial(kernel, n), out_shape=shapes, in_specs=[...]
where the time goes in v3:
time: 29.9 us; the launch traced here: 29.6 us
  Pallas kernels  29 us (97%)
  between operations  0.64 us (2%)
    pallas_call x1, Pallas kernels, body(): pl.pallas_call(functools.partial(kernel, n), out_shape=shapes, in_specs=[...  28 us
    pallas_call x1, Pallas kernels, body(): pl.pallas_call(hand_over, out_shape=shapes, in_specs=[vmem] * 4, out_spec...  1.03 us

profile of v3, /device:TPU:1, one launch (start us, length us, event | category | flops | bytes accessed | tf_op | source)
XLA Modules:
  0.0 29.6 jit_solution(12735644871242922572)
XLA Ops:
  0.6 28.0 %shard_map.84 = (bf16[256,1024]{1,0:T(8,128)(2,1)S(1)}, bf16[256,1024]{1,0:T(8,128)(2,1)S(1)}, bf16[256,128]{1,0:T(8,128)(2,1)S(1)}, bf16[256,128]{1,0:T(8,128)(2,1)S(1)}) custom-call(bf16[256,1024]{1,0:T(8,128)(2,1)} %q_hbm.1, bf16[256,1024]{1,0:T(8,128)(2,1)} %g_hbm.1, bf16[256,128]{1,0:T(8,128)(2,1)} %k_hbm.1, bf16[256,128]{1,0:T(8,128)(2,1)} %v_hbm.1, ...), custom_call_target="tpu_custom_call" | custom-call | tf_op jit(solution)/shard_map/pallas_call | solution.py:268
  28.6 1.0 %shard_map.85 = (bf16[256,1024]{1,0:T(8,128)(2,1)}, bf16[256,1024]{1,0:T(8,128)(2,1)}, bf16[256,128]{1,0:T(8,128)(2,1)}, bf16[256,128]{1,0:T(8,128)(2,1)}) custom-call(bf16[256,1024]{1,0:T(8,128)(2,1)S(1)} %get-tuple-element.8.refs_0_, bf16[256,1024]{1,0:T(8,128)(2,1)S(1)} %get-tuple-element.9.refs_1_, bf16[256,128]{1,0:T(8,128)(2,1)S(1)} %get-tuple-element.10.refs_2_, ...), custom_call_target="tpu_custom_call" | custom-call | tf_op jit(solution)/shard_map/pallas_call | solution.py:299

commit v4 on v3

--- a/solution.py
+++ b/solution.py
@@ -75,6 +75,61 @@
     me = lax.axis_index("ctx")
     reach = range(1, REACH + 1)
 
+    core = lax.rem(me, 2)
+    partner = me + 1 - 2 * core
+    apart = 3 - 2 * core
+    joint = 1 + 2 * core
+
+    barrier = pltpu.get_barrier_semaphore()
+
+    for d in (1, 3):
+
+        @pl.when(me >= d)
+        def _():
+            pl.semaphore_signal(barrier, inc=1, device_id={"ctx": me - d}, device_id_type=MESH)
+
+    @pl.when(me < n - 3)
+    def _():
+        pl.semaphore_wait(barrier, 2)
+
+    @pl.when((me >= n - 3) & (me < n - 1))
+    def _():
+        pl.semaphore_wait(barrier, 1)
+
+    def kv_moves(d, source=None, to=None):
+        pairs = ((k_hbm, keys), (v_hbm, values))
+        return [
+            pltpu.make_async_remote_copy(
+                src_ref=given if source is None else held.at[source],
+                dst_ref=held.at[REACH - d],
+                send_sem=kv_send.at[which, d - 1],
+                recv_sem=kv_recv.at[which, d - 1],
+                device_id={"ctx": me + d if to is None else to},
+                device_id_type=MESH,
+            )
+            for which, (given, held) in enumerate(pairs)
+        ]
+
+    def grad_move(d, to):
+        return pltpu.make_async_remote_copy(
+            src_ref=out_grad.at[d - 1],
+            dst_ref=in_grad.at[d - 1],
+            send_sem=grad_send.at[d - 1],
+            recv_sem=grad_recv.at[d - 1],
+            device_id={"ctx": to},
+            device_id_type=MESH,
+        )
+
+    @pl.when((core == 0) & (me + 3 < n))
+    def _():
+        for move in kv_moves(3):
+            move.start()
+
+    @pl.when(me + 1 < n)
+    def _():
+        for move in kv_moves(1):
+            move.start()
+
     local = []
     for slot in range(REACH + 1):
         block = lax.rem(me + n - REACH + slot, n)
@@ -88,13 +143,6 @@
     for copy in local:
         copy.start()
 
-    barrier = pltpu.get_barrier_semaphore()
-
-    def greet(there, other):
-        @pl.when(there)
-        def _():
-            pl.semaphore_signal(barrier, inc=1, device_id={"ctx": other}, device_id_type=MESH)
-
     for d in reach:
 
         @pl.when(me < d)
@@ -102,51 +150,12 @@
             keys[REACH - d] = jnp.zeros(keys.shape[1:], BF16)
             values[REACH - d] = jnp.zeros(values.shape[1:], BF16)
 
-    for d in reach:
-        greet(me >= d, me - d)
-    for missing in range(REACH):
-        here = me == n - 1 - REACH + missing if missing else me < n - REACH
-
-        @pl.when(here)
-        def _():
-            pl.semaphore_wait(barrier, REACH - missing)
-
-    def kv_moves(d):
-        return [
-            pltpu.make_async_remote_copy(
-                src_ref=source,
-                dst_ref=target.at[REACH - d],
-                send_sem=kv_send.at[which, d - 1],
-                recv_sem=kv_recv.at[which, d - 1],
-                device_id={"ctx": me + d},
-                device_id_type=MESH,
-            )
-            for which, (source, target) in enumerate(((k_hbm, keys), (v_hbm, values)))
-        ]
-
-    def grad_move(d):
-        return pltpu.make_async_remote_copy(
-            src_ref=out_grad.at[d - 1],
-            dst_ref=in_grad.at[d - 1],
-            send_sem=grad_send.at[d - 1],
-            recv_sem=grad_recv.at[d - 1],
-            device_id={"ctx": me - d},
-            device_id_type=MESH,
-        )
-
-    for d in reach:
-
-        @pl.when(me + d < n)
-        def _():
-            for move in kv_moves(d):
-                move.start()
-
+    stats[0] = jnp.full(stats.shape[1:], -1e30, F32)
+    stats[1] = jnp.zeros(stats.shape[1:], F32)
+    stats[2] = jnp.zeros(stats.shape[1:], F32)
     for copy in local[: REACH + 1]:
         copy.wait()
     fill_bias(doc, bias)
-    stats[0] = jnp.full(stats.shape[1:], -1e30, F32)
-    stats[1] = jnp.zeros(stats.shape[1:], F32)
-    stats[2] = jnp.zeros(stats.shape[1:], F32)
     for copy in local[REACH + 1 :]:
         copy.wait()
 
@@ -164,13 +173,40 @@
             slopes[j, :, columns] = slope
 
     first_pass(OWN)
-    for d in reach:
-
-        @pl.when(me >= d)
-        def _():
-            for move in kv_moves(d):
-                move.wait_recv()
-            first_pass(REACH - d)
+
+    @pl.when((core == 1) & (me + 3 < n))
+    def _():
+        for move in kv_moves(1):
+            move.wait_send()
+        for move in kv_moves(3):
+            move.start()
+
+    @pl.when(core == 1)
+    def _():
+        for move in kv_moves(1):
+            move.wait_recv()
+        first_pass(REACH - 1)
+
+    @pl.when(me >= joint)
+    def _():
+        taken = kv_moves(joint)
+        given = kv_moves(2, REACH - joint, partner)
+        for arrived, passed in zip(taken, given):
+            arrived.wait_recv()
+            passed.start()
+        first_pass(REACH - joint)
+
+    @pl.when(me >= 2)
+    def _():
+        for move in kv_moves(2):
+            move.wait_recv()
+        first_pass(REACH - 2)
+
+    @pl.when((core == 0) & (me >= 3))
+    def _():
+        for move in kv_moves(3):
+            move.wait_recv()
+        first_pass(REACH - 3)
 
     tops = [stats[0, j] for j in range(REACH + 1)]
     top = jnp.maximum(jnp.maximum(tops[0], tops[1]), jnp.maximum(tops[2], tops[3]))
@@ -193,19 +229,33 @@
         return dk, dv
 
     for d in reach:
-        j = REACH - d
-
-        @pl.when(me >= d)
-        def _():
-            dk, dv = second_pass(j)
-            out_grad[d - 1, 0] = dk.astype(BF16)
-            out_grad[d - 1, 1] = dv.astype(BF16)
-            grad_move(d).start()
 
         @pl.when(me < d)
         def _():
-            weights[j] = jnp.zeros(weights.shape[1:], BF16)
-            dscores[j] = jnp.zeros(dscores.shape[1:], BF16)
+            weights[REACH - d] = jnp.zeros(weights.shape[1:], BF16)
+            dscores[REACH - d] = jnp.zeros(dscores.shape[1:], BF16)
+
+    @pl.when(me >= 2)
+    def _():
+        dk, dv = second_pass(REACH - 2)
+        out_grad[1, 0] = dk.astype(BF16)
+        out_grad[1, 1] = dv.astype(BF16)
+        grad_move(2, partner).start()
+
+    @pl.when(me >= apart)
+    def _():
+        dk, dv = second_pass(REACH - apart)
+        out_grad[apart - 1, 0] = dk.astype(BF16)
+        out_grad[apart - 1, 1] = dv.astype(BF16)
+        grad_move(apart, me - apart).start()
+
+    @pl.when(me >= joint)
+    def _():
+        dk, dv = second_pass(REACH - joint)
+        grad_move(2, partner).wait_recv()
+        out_grad[joint - 1, 0] = (dk + in_grad[1, 0].astype(F32)).astype(BF16)
+        out_grad[joint - 1, 1] = (dv + in_grad[1, 1].astype(F32)).astype(BF16)
+        grad_move(joint, me - joint).start()
 
     dk, dv = second_pass(OWN)
     own_grad[0] = dk
@@ -220,19 +270,34 @@
         dq = sum(dot(keys_t[j], dscores[j, :, columns]) for j in range(REACH + 1)) * scale
         dq_ref[:, pl.ds(h * dim, dim)] = jnp.transpose(dq).astype(BF16)
 
-    for d in reach:
+    @pl.when((me + 1 < n) & ((core == 0) | (me + 3 >= n)))
+    def _():
+        for move in kv_moves(1):
+            move.wait_send()
+
+    @pl.when(me + 3 < n)
+    def _():
+        for move in kv_moves(3):
+            move.wait_send()
+
+    @pl.when(me >= joint)
+    def _():
+        for move in kv_moves(2, REACH - joint, partner):
+            move.wait_send()
+        grad_move(2, partner).wait_send()
+        grad_move(joint, me - joint).wait_send()
+
+    @pl.when(me >= apart)
+    def _():
+        grad_move(apart, me - apart).wait_send()
+
+    for d in (1, 3):
 
         @pl.when(me + d < n)
         def _():
-            for move in kv_moves(d):
-                move.wait_send()
-            grad_move(d).wait_recv()
+            grad_move(d, me).wait_recv()
             for which in range(2):
                 own_grad[which] += in_grad[d - 1, which].astype(F32)
-
-        @pl.when(me >= d)
-        def _():
-            grad_move(d).wait_send()
 
     dk_ref[...] = own_grad[0].astype(BF16)
     dv_ref[...] = own_grad[1].astype(BF16)

time: 29.9 us -> 30.4 us (1.017)
  Pallas kernels: 29 us -> 29.5 us
    pallas_call x1, Pallas kernels: 28 us -> 28.5 us  [body(): pl.pallas_call(functools.partial(kernel, n), out_shape=shapes, in_specs=[...]
where the time goes in v4:
time: 30.4 us; the launch traced here: 30.1 us
  Pallas kernels  29.5 us (97%)
  between operations  0.64 us (2%)
    pallas_call x1, Pallas kernels, body(): pl.pallas_call(functools.partial(kernel, n), out_shape=shapes, in_specs=[...  28.5 us
    pallas_call x1, Pallas kernels, body(): pl.pallas_call(hand_over, out_shape=shapes, in_specs=[vmem] * 4, out_spec...  1.03 us

profile of v4, /device:TPU:1, one launch (start us, length us, event | category | flops | bytes accessed | tf_op | source)
XLA Modules:
  0.0 30.1 jit_solution(6085006829572185732)
XLA Ops:
  0.6 28.5 %shard_map.84 = (bf16[256,1024]{1,0:T(8,128)(2,1)S(1)}, bf16[256,1024]{1,0:T(8,128)(2,1)S(1)}, bf16[256,128]{1,0:T(8,128)(2,1)S(1)}, bf16[256,128]{1,0:T(8,128)(2,1)S(1)}) custom-call(bf16[256,1024]{1,0:T(8,128)(2,1)} %q_hbm.1, bf16[256,1024]{1,0:T(8,128)(2,1)} %g_hbm.1, bf16[256,128]{1,0:T(8,128)(2,1)} %k_hbm.1, bf16[256,128]{1,0:T(8,128)(2,1)} %v_hbm.1, ...), custom_call_target="tpu_custom_call" | custom-call | tf_op jit(solution)/shard_map/pallas_call | solution.py:333
  29.1 1.0 %shard_map.85 = (bf16[256,1024]{1,0:T(8,128)(2,1)}, bf16[256,1024]{1,0:T(8,128)(2,1)}, bf16[256,128]{1,0:T(8,128)(2,1)}, bf16[256,128]{1,0:T(8,128)(2,1)}) custom-call(bf16[256,1024]{1,0:T(8,128)(2,1)S(1)} %get-tuple-element.8.refs_0_, bf16[256,1024]{1,0:T(8,128)(2,1)S(1)} %get-tuple-element.9.refs_1_, bf16[256,128]{1,0:T(8,128)(2,1)S(1)} %get-tuple-element.10.refs_2_, ...), custom_call_target="tpu_custom_call" | custom-call | tf_op jit(solution)/shard_map/pallas_call | solution.py:364

commit v5 on v4

--- a/solution.py
+++ b/solution.py
@@ -61,6 +61,7 @@
     weights,
     dscores,
     own_grad,
+    pending,
     out_grad,
     in_grad,
     local_sem,
@@ -110,12 +111,12 @@
             for which, (given, held) in enumerate(pairs)
         ]
 
-    def grad_move(d, to):
+    def grad_move(which, d, to):
         return pltpu.make_async_remote_copy(
-            src_ref=out_grad.at[d - 1],
-            dst_ref=in_grad.at[d - 1],
-            send_sem=grad_send.at[d - 1],
-            recv_sem=grad_recv.at[d - 1],
+            src_ref=out_grad.at[d - 1, which],
+            dst_ref=in_grad.at[d - 1, which],
+            send_sem=grad_send.at[d - 1, which],
+            recv_sem=grad_recv.at[d - 1, which],
             device_id={"ctx": to},
             device_id_type=MESH,
         )
@@ -159,17 +160,23 @@
     for copy in local[REACH + 1 :]:
         copy.wait()
 
-    def first_pass(j):
+    def first_pass(j, keys_here=None, values_here=None):
+        if keys_here is not None:
+            keys_here()
         for h in range(heads):
             columns = pl.ds(h * rows, rows)
             s = dot(keys[j], q[h], NT) + bias[j]
             top = s.max(axis=0, keepdims=True)
             e = jnp.exp2((s - top) * exponent)
-            slope = dot(values[j], g[h], NT)
             stats[0, j, h : h + 1, :] = top
             stats[1, j, h : h + 1, :] = e.sum(axis=0, keepdims=True)
-            stats[2, j, h : h + 1, :] = (e * slope).sum(axis=0, keepdims=True)
             raw[j, :, columns] = e
+        if values_here is not None:
+            values_here()
+        for h in range(heads):
+            columns = pl.ds(h * rows, rows)
+            slope = dot(values[j], g[h], NT)
+            stats[2, j, h : h + 1, :] = (raw[j, :, columns] * slope).sum(axis=0, keepdims=True)
             slopes[j, :, columns] = slope
 
     first_pass(OWN)
@@ -183,30 +190,26 @@
 
     @pl.when(core == 1)
     def _():
-        for move in kv_moves(1):
+        first_pass(REACH - 1, *(move.wait_recv for move in kv_moves(1)))
+
+    @pl.when(me >= joint)
+    def _():
+        given = kv_moves(2, REACH - joint, partner)
+
+        def arrive(which, move):
             move.wait_recv()
-        first_pass(REACH - 1)
-
-    @pl.when(me >= joint)
-    def _():
-        taken = kv_moves(joint)
-        given = kv_moves(2, REACH - joint, partner)
-        for arrived, passed in zip(taken, given):
-            arrived.wait_recv()
-            passed.start()
-        first_pass(REACH - joint)
+            given[which].start()
+
+        steps = [functools.partial(arrive, i, move) for i, move in enumerate(kv_moves(joint))]
+        first_pass(REACH - joint, *steps)
 
     @pl.when(me >= 2)
     def _():
-        for move in kv_moves(2):
-            move.wait_recv()
-        first_pass(REACH - 2)
+        first_pass(REACH - 2, *(move.wait_recv for move in kv_moves(2)))
 
     @pl.when((core == 0) & (me >= 3))
     def _():
-        for move in kv_moves(3):
-            move.wait_recv()
-        first_pass(REACH - 3)
+        first_pass(REACH - 3, *(move.wait_recv for move in kv_moves(3)))
 
     tops = [stats[0, j] for j in range(REACH + 1)]
     top = jnp.maximum(jnp.maximum(tops[0], tops[1]), jnp.maximum(tops[2], tops[3]))
@@ -217,16 +220,18 @@
         factors[j] = grown[j] * inverse
     factors[REACH + 1] = delta
 
-    def second_pass(j):
+    def second_pass(j, take):
         for h in range(heads):
             columns = pl.ds(h * rows, rows)
             w = raw[j, :, columns] * factors[j, h : h + 1, :]
             weights[j, :, columns] = w.astype(BF16)
-            ds = w * (slopes[j, :, columns] - factors[REACH + 1, h : h + 1, :])
-            dscores[j, :, columns] = ds.astype(BF16)
-        dv = dot(weights[j], g[...].reshape(heads * rows, dim))
-        dk = dot(dscores[j], q[...].reshape(heads * rows, dim)) * scale
-        return dk, dv
+        take(1, dot(weights[j], g[...].reshape(heads * rows, dim)))
+        for h in range(heads):
+            columns = pl.ds(h * rows, rows)
+            w = raw[j, :, columns] * factors[j, h : h + 1, :]
+            slope = slopes[j, :, columns] - factors[REACH + 1, h : h + 1, :]
+            dscores[j, :, columns] = (w * slope).astype(BF16)
+        take(0, dot(dscores[j], q[...].reshape(heads * rows, dim)) * scale)
 
     for d in reach:
 
@@ -235,31 +240,50 @@
             weights[REACH - d] = jnp.zeros(weights.shape[1:], BF16)
             dscores[REACH - d] = jnp.zeros(dscores.shape[1:], BF16)
 
-    @pl.when(me >= 2)
-    def _():
-        dk, dv = second_pass(REACH - 2)
-        out_grad[1, 0] = dk.astype(BF16)
-        out_grad[1, 1] = dv.astype(BF16)
-        grad_move(2, partner).start()
-
-    @pl.when(me >= apart)
-    def _():
-        dk, dv = second_pass(REACH - apart)
-        out_grad[apart - 1, 0] = dk.astype(BF16)
-        out_grad[apart - 1, 1] = dv.astype(BF16)
-        grad_move(apart, me - apart).start()
-
-    @pl.when(me >= joint)
-    def _():
-        dk, dv = second_pass(REACH - joint)
-        grad_move(2, partner).wait_recv()
-        out_grad[joint - 1, 0] = (dk + in_grad[1, 0].astype(F32)).astype(BF16)
-        out_grad[joint - 1, 1] = (dv + in_grad[1, 1].astype(F32)).astype(BF16)
-        grad_move(joint, me - joint).start()
-
-    dk, dv = second_pass(OWN)
-    own_grad[0] = dk
-    own_grad[1] = dv
+    def alone(d, to):
+        def take(which, grad):
+            out_grad[d - 1, which] = grad.astype(BF16)
+            grad_move(which, d, to).start()
+
+        second_pass(REACH - d, take)
+
+    def hold(which, grad):
+        pending[which] = grad
+
+    def join(d):
+        for which in (1, 0):
+            grad_move(which, 2, partner).wait_recv()
+            total = pending[which] + in_grad[1, which].astype(F32)
+            out_grad[d - 1, which] = total.astype(BF16)
+            grad_move(which, d, me - d).start()
+
+    def keep(which, grad):
+        own_grad[which] = grad
+
+    @pl.when((core == 0) & (me >= 2))
+    def _():
+        second_pass(REACH - 1, hold)
+        alone(2, partner)
+        join(1)
+
+    @pl.when((core == 0) & (me >= 3))
+    def _():
+        alone(3, me - 3)
+
+    @pl.when((core == 1) & (me >= 3))
+    def _():
+        alone(2, partner)
+        second_pass(REACH - 3, hold)
+
+    @pl.when(core == 1)
+    def _():
+        alone(1, me - 1)
+
+    @pl.when((core == 1) & (me >= 3))
+    def _():
+        join(3)
+
+    second_pass(OWN, keep)
 
     keys_t = [jnp.transpose(keys[j]) for j in range(REACH + 1)]
     values_t = [jnp.transpose(values[j]) for j in range(REACH + 1)]
@@ -284,19 +308,21 @@
     def _():
         for move in kv_moves(2, REACH - joint, partner):
             move.wait_send()
-        grad_move(2, partner).wait_send()
-        grad_move(joint, me - joint).wait_send()
+        for which in range(2):
+            grad_move(which, 2, partner).wait_send()
+            grad_move(which, joint, me - joint).wait_send()
 
     @pl.when(me >= apart)
     def _():
-        grad_move(apart, me - apart).wait_send()
-
-    for d in (1, 3):
+        for which in range(2):
+            grad_move(which, apart, me - apart).wait_send()
+
+    for d in (3, 1):
 
         @pl.when(me + d < n)
         def _():
-            grad_move(d, me).wait_recv()
-            for which in range(2):
+            for which in (1, 0):
+                grad_move(which, d, me).wait_recv()
                 own_grad[which] += in_grad[d - 1, which].astype(F32)
 
     dk_ref[...] = own_grad[0].astype(BF16)
@@ -349,13 +375,14 @@
             pltpu.VMEM((blocks, rows, heads * rows), BF16),
             pltpu.VMEM((blocks, rows, heads * rows), BF16),
             pltpu.VMEM((2, rows, dim), F32),
+            pltpu.VMEM((2, rows, dim), F32),
             pltpu.VMEM((REACH, 2, rows, dim), BF16),
             pltpu.VMEM((REACH, 2, rows, dim), BF16),
             pltpu.SemaphoreType.DMA((3, 8)),
             pltpu.SemaphoreType.DMA((2, REACH)),
             pltpu.SemaphoreType.DMA((2, REACH)),
-            pltpu.SemaphoreType.DMA((REACH,)),
-            pltpu.SemaphoreType.DMA((REACH,)),
+            pltpu.SemaphoreType.DMA((REACH, 2)),
+            pltpu.SemaphoreType.DMA((REACH, 2)),
         ],
         compiler_params=pltpu.CompilerParams(
             collective_id=0, has_side_effects=True, vmem_limit_bytes=48 << 20

time: 30.4 us -> 28.9 us (0.951)
  Pallas kernels: 29.5 us -> 28.1 us
    pallas_call x1, Pallas kernels: 28.5 us -> 27 us  [body(): pl.pallas_call(functools.partial(kernel, n), out_shape=shapes, in_specs=[...]
where the time goes in v5:
time: 28.9 us; the launch traced here: 28.7 us
  Pallas kernels  28.1 us (97%)
  between operations  0.64 us (2%)
    pallas_call x1, Pallas kernels, body(): pl.pallas_call(functools.partial(kernel, n), out_shape=shapes, in_specs=[...  27 us
    pallas_call x1, Pallas kernels, body(): pl.pallas_call(hand_over, out_shape=shapes, in_specs=[vmem] * 4, out_spec...  1.03 us

profile of v5, /device:TPU:1, one launch (start us, length us, event | category | flops | bytes accessed | tf_op | source)
XLA Modules:
  0.0 28.7 jit_solution(6198443178979723132)
XLA Ops:
  0.6 27.0 %shard_map.84 = (bf16[256,1024]{1,0:T(8,128)(2,1)S(1)}, bf16[256,1024]{1,0:T(8,128)(2,1)S(1)}, bf16[256,128]{1,0:T(8,128)(2,1)S(1)}, bf16[256,128]{1,0:T(8,128)(2,1)S(1)}) custom-call(bf16[256,1024]{1,0:T(8,128)(2,1)} %q_hbm.1, bf16[256,1024]{1,0:T(8,128)(2,1)} %g_hbm.1, bf16[256,128]{1,0:T(8,128)(2,1)} %k_hbm.1, bf16[256,128]{1,0:T(8,128)(2,1)} %v_hbm.1, ...), custom_call_target="tpu_custom_call" | custom-call | tf_op jit(solution)/shard_map/pallas_call | solution.py:359
  27.7 1.0 %shard_map.85 = (bf16[256,1024]{1,0:T(8,128)(2,1)}, bf16[256,1024]{1,0:T(8,128)(2,1)}, bf16[256,128]{1,0:T(8,128)(2,1)}, bf16[256,128]{1,0:T(8,128)(2,1)}) custom-call(bf16[256,1024]{1,0:T(8,128)(2,1)S(1)} %get-tuple-element.8.refs_0_, bf16[256,1024]{1,0:T(8,128)(2,1)S(1)} %get-tuple-element.9.refs_1_, bf16[256,128]{1,0:T(8,128)(2,1)S(1)} %get-tuple-element.10.refs_2_, ...), custom_call_target="tpu_custom_call" | custom-call | tf_op jit(solution)/shard_map/pallas_call | solution.py:391

commit v6 on v5

--- a/solution.py
+++ b/solution.py
@@ -192,20 +192,23 @@
     def _():
         first_pass(REACH - 1, *(move.wait_recv for move in kv_moves(1)))
 
-    @pl.when(me >= joint)
-    def _():
-        given = kv_moves(2, REACH - joint, partner)
-
-        def arrive(which, move):
-            move.wait_recv()
-            given[which].start()
-
-        steps = [functools.partial(arrive, i, move) for i, move in enumerate(kv_moves(joint))]
-        first_pass(REACH - joint, *steps)
-
-    @pl.when(me >= 2)
-    def _():
-        first_pass(REACH - 2, *(move.wait_recv for move in kv_moves(2)))
+    early = core * (4 // (me + 1))
+    first = joint + early * (2 - joint)
+    for d in (first, joint + 2 - first):
+
+        @pl.when(me >= 2)
+        def _():
+            given = kv_moves(2, REACH - joint, partner)
+
+            def arrive(which, move):
+                move.wait_recv()
+
+                @pl.when(d == joint)
+                def _():
+                    given[which].start()
+
+            steps = [functools.partial(arrive, i, move) for i, move in enumerate(kv_moves(d))]
+            first_pass(REACH - d, *steps)
 
     @pl.when((core == 0) & (me >= 3))
     def _():
@@ -263,7 +266,17 @@
     @pl.when((core == 0) & (me >= 2))
     def _():
         second_pass(REACH - 1, hold)
+
+    @pl.when(me == 2)
+    def _():
+        join(1)
+
+    @pl.when((core == 0) & (me >= 2))
+    def _():
         alone(2, partner)
+
+    @pl.when((core == 0) & (me > 2))
+    def _():
         join(1)
 
     @pl.when((core == 0) & (me >= 3))

time: 28.9 us -> 27.8 us (0.962)
  Pallas kernels: 28.1 us -> 26.9 us
    pallas_call x1, Pallas kernels: 27 us -> 25.9 us  [body(): pl.pallas_call(functools.partial(kernel, n), out_shape=shapes, in_specs=[...]
where the time goes in v6:
time: 27.8 us; the launch traced here: 27.6 us
  Pallas kernels  26.9 us (97%)
  between operations  0.64 us (2%)
    pallas_call x1, Pallas kernels, body(): pl.pallas_call(functools.partial(kernel, n), out_shape=shapes, in_specs=[...  25.9 us
    pallas_call x1, Pallas kernels, body(): pl.pallas_call(hand_over, out_shape=shapes, in_specs=[vmem] * 4, out_spec...  1.03 us

profile of v6, /device:TPU:1, one launch (start us, length us, event | category | flops | bytes accessed | tf_op | source)
XLA Modules:
  0.0 27.6 jit_solution(16870333853076895381)
XLA Ops:
  0.6 25.9 %shard_map.84 = (bf16[256,1024]{1,0:T(8,128)(2,1)S(1)}, bf16[256,1024]{1,0:T(8,128)(2,1)S(1)}, bf16[256,128]{1,0:T(8,128)(2,1)S(1)}, bf16[256,128]{1,0:T(8,128)(2,1)S(1)}) custom-call(bf16[256,1024]{1,0:T(8,128)(2,1)} %q_hbm.1, bf16[256,1024]{1,0:T(8,128)(2,1)} %g_hbm.1, bf16[256,128]{1,0:T(8,128)(2,1)} %k_hbm.1, bf16[256,128]{1,0:T(8,128)(2,1)} %v_hbm.1, ...), custom_call_target="tpu_custom_call" | custom-call | tf_op jit(solution)/shard_map/pallas_call | solution.py:372
  26.5 1.0 %shard_map.85 = (bf16[256,1024]{1,0:T(8,128)(2,1)}, bf16[256,1024]{1,0:T(8,128)(2,1)}, bf16[256,128]{1,0:T(8,128)(2,1)}, bf16[256,128]{1,0:T(8,128)(2,1)}) custom-call(bf16[256,1024]{1,0:T(8,128)(2,1)S(1)} %get-tuple-element.8.refs_0_, bf16[256,1024]{1,0:T(8,128)(2,1)S(1)} %get-tuple-element.9.refs_1_, bf16[256,128]{1,0:T(8,128)(2,1)S(1)} %get-tuple-element.10.refs_2_, ...), custom_call_target="tpu_custom_call" | custom-call | tf_op jit(solution)/shard_map/pallas_call | solution.py:404

commit v7 on v5

--- a/solution.py
+++ b/solution.py
@@ -160,9 +160,7 @@
     for copy in local[REACH + 1 :]:
         copy.wait()
 
-    def first_pass(j, keys_here=None, values_here=None):
-        if keys_here is not None:
-            keys_here()
+    def key_pass(j):
         for h in range(heads):
             columns = pl.ds(h * rows, rows)
             s = dot(keys[j], q[h], NT) + bias[j]
@@ -171,15 +169,26 @@
             stats[0, j, h : h + 1, :] = top
             stats[1, j, h : h + 1, :] = e.sum(axis=0, keepdims=True)
             raw[j, :, columns] = e
-        if values_here is not None:
-            values_here()
+
+    def value_pass(j):
         for h in range(heads):
             columns = pl.ds(h * rows, rows)
             slope = dot(values[j], g[h], NT)
             stats[2, j, h : h + 1, :] = (raw[j, :, columns] * slope).sum(axis=0, keepdims=True)
             slopes[j, :, columns] = slope
 
-    first_pass(OWN)
+    def arrive(which, d, passing=False):
+        kv_moves(d)[which].wait_recv()
+        if passing:
+
+            @pl.when(d == joint)
+            def _():
+                kv_moves(2, REACH - joint, partner)[which].start()
+
+        (key_pass, value_pass)[which](REACH - d)
+
+    key_pass(OWN)
+    value_pass(OWN)
 
     @pl.when((core == 1) & (me + 3 < n))
     def _():
@@ -190,42 +199,38 @@
 
     @pl.when(core == 1)
     def _():
-        first_pass(REACH - 1, *(move.wait_recv for move in kv_moves(1)))
-
-    @pl.when(me >= joint)
-    def _():
-        given = kv_moves(2, REACH - joint, partner)
-
-        def arrive(which, move):
-            move.wait_recv()
-            given[which].start()
-
-        steps = [functools.partial(arrive, i, move) for i, move in enumerate(kv_moves(joint))]
-        first_pass(REACH - joint, *steps)
+        arrive(0, 1)
+        arrive(1, 1)
+
+    early = core * (4 // (me + 1))
+    first = joint + early * (2 - joint)
+    second = joint + 2 - first
 
     @pl.when(me >= 2)
     def _():
-        first_pass(REACH - 2, *(move.wait_recv for move in kv_moves(2)))
+        arrive(0, first, True)
+        arrive(1, first, True)
+        arrive(0, second, True)
 
     @pl.when((core == 0) & (me >= 3))
     def _():
-        first_pass(REACH - 3, *(move.wait_recv for move in kv_moves(3)))
+        arrive(0, 3)
 
     tops = [stats[0, j] for j in range(REACH + 1)]
     top = jnp.maximum(jnp.maximum(tops[0], tops[1]), jnp.maximum(tops[2], tops[3]))
     grown = [jnp.exp2((x - top) * exponent) for x in tops]
     inverse = 1.0 / sum(x * stats[1, j] for j, x in enumerate(grown))
-    delta = sum(x * stats[2, j] for j, x in enumerate(grown)) * inverse
     for j in range(REACH + 1):
         factors[j] = grown[j] * inverse
-    factors[REACH + 1] = delta
-
-    def second_pass(j, take):
+
+    def weight_pass(j, take):
         for h in range(heads):
             columns = pl.ds(h * rows, rows)
             w = raw[j, :, columns] * factors[j, h : h + 1, :]
             weights[j, :, columns] = w.astype(BF16)
         take(1, dot(weights[j], g[...].reshape(heads * rows, dim)))
+
+    def score_pass(j, take):
         for h in range(heads):
             columns = pl.ds(h * rows, rows)
             w = raw[j, :, columns] * factors[j, h : h + 1, :]
@@ -233,6 +238,10 @@
             dscores[j, :, columns] = (w * slope).astype(BF16)
         take(0, dot(dscores[j], q[...].reshape(heads * rows, dim)) * scale)
 
+    def second_pass(j, take):
+        weight_pass(j, take)
+        score_pass(j, take)
+
     for d in reach:
 
         @pl.when(me < d)
@@ -240,48 +249,73 @@
             weights[REACH - d] = jnp.zeros(weights.shape[1:], BF16)
             dscores[REACH - d] = jnp.zeros(dscores.shape[1:], BF16)
 
-    def alone(d, to):
+    def away(d, to):
         def take(which, grad):
             out_grad[d - 1, which] = grad.astype(BF16)
             grad_move(which, d, to).start()
 
-        second_pass(REACH - d, take)
+        return take
 
     def hold(which, grad):
         pending[which] = grad
 
-    def join(d):
-        for which in (1, 0):
-            grad_move(which, 2, partner).wait_recv()
-            total = pending[which] + in_grad[1, which].astype(F32)
-            out_grad[d - 1, which] = total.astype(BF16)
-            grad_move(which, d, me - d).start()
+    def join(d, which):
+        grad_move(which, 2, partner).wait_recv()
+        total = pending[which] + in_grad[1, which].astype(F32)
+        out_grad[d - 1, which] = total.astype(BF16)
+        grad_move(which, d, me - d).start()
 
     def keep(which, grad):
         own_grad[which] = grad
 
+    def lead(step, which):
+        @pl.when((core == 0) & (me >= 2))
+        def _():
+            step(REACH - 1, hold)
+
+        @pl.when(me == 2)
+        def _():
+            join(1, which)
+
+        @pl.when((core == 1) & (me >= 3))
+        def _():
+            step(REACH - 2, away(2, partner))
+
+    lead(weight_pass, 1)
+
+    @pl.when(me >= 2)
+    def _():
+        arrive(1, second, True)
+
+    @pl.when((core == 0) & (me >= 3))
+    def _():
+        arrive(1, 3)
+
+    factors[REACH + 1] = sum(factors[j] * stats[2, j] for j in range(REACH + 1))
+    lead(score_pass, 0)
+
     @pl.when((core == 0) & (me >= 2))
     def _():
-        second_pass(REACH - 1, hold)
-        alone(2, partner)
-        join(1)
-
-    @pl.when((core == 0) & (me >= 3))
-    def _():
-        alone(3, me - 3)
+        second_pass(REACH - 2, away(2, partner))
+
+    @pl.when((core == 0) & (me > 2))
+    def _():
+        join(1, 1)
+        join(1, 0)
+        second_pass(REACH - 3, away(3, me - 3))
 
     @pl.when((core == 1) & (me >= 3))
     def _():
-        alone(2, partner)
         second_pass(REACH - 3, hold)
 
     @pl.when(core == 1)
     def _():
-        alone(1, me - 1)
+        second_pass(REACH - 1, away(1, me - 1))
 
     @pl.when((core == 1) & (me >= 3))
     def _():
-        join(3)
+        join(3, 1)
+        join(3, 0)
 
     second_pass(OWN, keep)
 

time: 28.9 us -> 26.6 us (0.920)
  Pallas kernels: 28.1 us -> 25.8 us
    pallas_call x1, Pallas kernels: 27 us -> 24.7 us  [body(): pl.pallas_call(functools.partial(kernel, n), out_shape=shapes, in_specs=[...]
where the time goes in v7:
time: 26.6 us; the launch traced here: 26.4 us
  Pallas kernels  25.8 us (97%)
  between operations  0.64 us (2%)
    pallas_call x1, Pallas kernels, body(): pl.pallas_call(functools.partial(kernel, n), out_shape=shapes, in_specs=[...  24.7 us
    pallas_call x1, Pallas kernels, body(): pl.pallas_call(hand_over, out_shape=shapes, in_specs=[vmem] * 4, out_spec...  1.03 us

profile of v7, /device:TPU:1, one launch (start us, length us, event | category | flops | bytes accessed | tf_op | source)
XLA Modules:
  0.0 26.4 jit_solution(17368862280106179143)
XLA Ops:
  0.6 24.7 %shard_map.84 = (bf16[256,1024]{1,0:T(8,128)(2,1)S(1)}, bf16[256,1024]{1,0:T(8,128)(2,1)S(1)}, bf16[256,128]{1,0:T(8,128)(2,1)S(1)}, bf16[256,128]{1,0:T(8,128)(2,1)S(1)}) custom-call(bf16[256,1024]{1,0:T(8,128)(2,1)} %q_hbm.1, bf16[256,1024]{1,0:T(8,128)(2,1)} %g_hbm.1, bf16[256,128]{1,0:T(8,128)(2,1)} %k_hbm.1, bf16[256,128]{1,0:T(8,128)(2,1)} %v_hbm.1, ...), custom_call_target="tpu_custom_call" | custom-call | tf_op jit(solution)/shard_map/pallas_call | solution.py:393
  25.4 1.0 %shard_map.85 = (bf16[256,1024]{1,0:T(8,128)(2,1)}, bf16[256,1024]{1,0:T(8,128)(2,1)}, bf16[256,128]{1,0:T(8,128)(2,1)}, bf16[256,128]{1,0:T(8,128)(2,1)}) custom-call(bf16[256,1024]{1,0:T(8,128)(2,1)S(1)} %get-tuple-element.8.refs_0_, bf16[256,1024]{1,0:T(8,128)(2,1)S(1)} %get-tuple-element.9.refs_1_, bf16[256,128]{1,0:T(8,128)(2,1)S(1)} %get-tuple-element.10.refs_2_, ...), custom_call_target="tpu_custom_call" | custom-call | tf_op jit(solution)/shard_map/pallas_call | solution.py:425
